TPU v7x, 32 devices: a whole 2x2x4 slice. The times are simulated.
32 devices in a mesh: dp: 8 (over z, x), shard: 4 (over y, core).
Axes of the slice: x: 2, y: 2, z: 4, core: 2. Of those that a mesh axis runs over, the one named last changes fastest.
Arguments:
- noisy: float32 [128, 256, 16], P(('dp', 'shard')), may hold values from -6 to 6
- velocity: float32 [128, 256, 16], P(('dp', 'shard')), may hold values from -6 to 6
- tstep_idx: int32 [128], P(('dp', 'shard')), may hold values from 0 to 999
- class_ids: int32 [128], P(('dp', 'shard')), may hold values from 0 to 1000
- time_weight: float32 [128], P(('dp', 'shard')), may hold values from 0.3 to 3
- dino: bfloat16 [128, 256, 768], P(('dp', 'shard')), may hold values from -6 to 6
- owner_map: int32 [12], replicated, may hold values from 0 to 11, each once
- adam_flat: float32 [2129920], P(('dp', 'shard')), may hold values from -4 to 4
- adam_m: float32 [2129920], P(('dp', 'shard')), may hold values from -0.015625 to 0.015625
- adam_v: float32 [2129920], P(('dp', 'shard')), may hold values from 1e-06 to 0.0001
- blocks_w: float32 [12, 384, 384], P('shard'), may hold values from -0.3125 to 0.3125
- stat_left: float32 [12, 384, 384], P('shard'), may hold values from -0.005 to 0.01, as said below
- stat_right: float32 [12, 384, 384], P('shard'), may hold values from -0.005 to 0.01, as said below
- root_left: float32 [12, 384, 384], P('shard'), may hold values from -3 to 3, as said below
- root_right: float32 [12, 384, 384], P('shard'), may hold values from -3 to 3, as said below
Outputs:
- loss: float32 [], replicated
- block_update: float32 [12, 384, 384], P('shard')
- stat_left_new: float32 [12, 384, 384], P('shard')
- stat_right_new: float32 [12, 384, 384], P('shard')
- adam_update: float32 [2129920], P(('dp', 'shard'))
- adam_m_new: float32 [2129920], P(('dp', 'shard'))
- adam_v_new: float32 [2129920], P(('dp', 'shard'))
Inputs may be any that keep to these rules, and one draw needn't show every extreme that they name: `owner_map`: each block number appears once. `stat_left`: each slot is symmetric positive definite. `stat_right`: each slot is symmetric positive definite. `root_left`: each slot is symmetric positive definite. `root_right`: each slot is symmetric positive definite.
All inputs are finite; a program needn't handle non-finite values.
Results may differ from a plain program's by a relative error of at most 0.0097.
Values may be sent and summed in bfloat16 or wider, within the bound.
No kernel may reach another device: no remote copies, remote signals or barrier semaphores. Data moves between devices by JAX's collectives and lax.ppermute only.
A program may use at most 192 MiB of HBM per device.

v0:
```python
import functools
import math
import jax
import jax.numpy as jnp
from jax import lax
from jax.sharding import PartitionSpec as P

D = 384
HEADS = 6
HDIM = 64
F = 1536
PD = 16
GRID = 16
SEQ = 256
FREQ = 256
NCLS = 1001
DINO = 768
STEP = 10
NBLK = 12
ADAM_LEN = 2125072
ADAM_PAD = 2129920
HIGHEST = lax.Precision.HIGHEST
BETA_ONE = 0.9
BETA_TWO = 0.95
ADAM_EPS = 1e-08
ADAM_RATE = 0.01
DECAY_RATE = 0.1
STAT_BETA = 0.9
SHAMPOO_RATE = 0.02
RMS_EPS = 1e-08
REPA_WEIGHT = 0.5
NORM_EPS = 1e-06


def segment_shapes():
    return [
        (PD, D),
        (D,),
        (FREQ, D),
        (D,),
        (D, D),
        (D,),
        (NCLS, D),
        (D, 6 * D),
        (6 * D,),
        (D,),
        (D,),
        (D,),
        (F,),
        (D,),
        (D, 2 * D),
        (2 * D,),
        (D, PD),
        (PD,),
        (D, DINO),
        (DINO,),
    ]


def unflatten(flat):
    pieces = []
    offset = 0
    for seg_dims in segment_shapes():
        length = math.prod(seg_dims)
        pieces.append(flat[offset : offset + length].reshape(seg_dims))
        offset += length
    return pieces


def position_table():
    quarter = D // 4
    frequencies = 1.0 / 10000.0 ** (jnp.arange(quarter, dtype=jnp.float32) / quarter)
    cell_ids = jnp.arange(SEQ, dtype=jnp.int32)
    row_arg = (cell_ids // GRID).astype(jnp.float32)[:, None] * frequencies[None, :]
    col_arg = (cell_ids % GRID).astype(jnp.float32)[:, None] * frequencies[None, :]
    return jnp.concatenate(
        [jnp.sin(col_arg), jnp.cos(col_arg), jnp.sin(row_arg), jnp.cos(row_arg)], axis=1
    )


def time_features(tstep_idx):
    half_freq = FREQ // 2
    frequencies = jnp.exp(-math.log(10000.0) * jnp.arange(half_freq, dtype=jnp.float32) / half_freq)
    angles = (tstep_idx.astype(jnp.float32) + 0.5)[:, None] * frequencies[None, :]
    return jnp.concatenate([jnp.cos(angles), jnp.sin(angles)], axis=1)


def normalize(values):
    centered = values - jnp.mean(values, axis=-1, keepdims=True)
    inv_dev = lax.rsqrt(jnp.mean(centered * centered, axis=-1, keepdims=True) + NORM_EPS)
    return (centered * inv_dev, inv_dev)


def normalize_back(grad_in, normed, inv_dev):
    return inv_dev * (
        grad_in
        - jnp.mean(grad_in, axis=-1, keepdims=True)
        - normed * jnp.mean(grad_in * normed, axis=-1, keepdims=True)
    )


def condition_terms(
    tstep_idx,
    class_ids,
    time_in_weight,
    time_in_bias,
    time_out_weight,
    time_out_bias,
    class_table,
    mod_weight,
    mod_bias,
    final_mod_weight,
    final_mod_bias,
):
    features = time_features(tstep_idx)
    time_hidden = jax.nn.silu(jnp.dot(features, time_in_weight, precision=HIGHEST) + time_in_bias)
    onehot_class = (class_ids[:, None] == jnp.arange(NCLS, dtype=jnp.int32)[None, :]).astype(
        jnp.float32
    )
    condition = (
        jnp.dot(time_hidden, time_out_weight, precision=HIGHEST)
        + time_out_bias
        + jnp.dot(onehot_class, class_table, precision=HIGHEST)
    )
    cond_act = jax.nn.silu(condition)
    modulation = jnp.dot(cond_act, mod_weight, precision=HIGHEST) + mod_bias
    final_mods = jnp.dot(cond_act, final_mod_weight, precision=HIGHEST) + final_mod_bias
    return (modulation, final_mods)


def cosine_total(aligned, dino_f):
    products = jnp.sum(aligned * dino_f, axis=-1)
    return jnp.sum(
        products
        * lax.rsqrt(jnp.sum(aligned * aligned, axis=-1) + NORM_EPS)
        * lax.rsqrt(jnp.sum(dino_f * dino_f, axis=-1) + NORM_EPS)
    )


def matmul(left, right):
    return jnp.dot(left, right, preferred_element_type=jnp.float32)


def row_total(rounded):
    return jnp.sum(rounded.astype(jnp.float32), axis=0)


def body(
    noisy,
    velocity,
    tstep_idx,
    class_ids,
    time_weight,
    dino,
    owner_map,
    adam_flat,
    adam_m,
    adam_v,
    blocks_w,
    stat_left,
    stat_right,
    root_left,
    root_right,
):
    devices = lax.axis_size("dp") * lax.axis_size("shard")
    images = noisy.shape[0]
    seq = noisy.shape[1]
    total_img = images * devices
    rows = images * seq
    fc_ratio = F // D
    flat_low = lax.all_gather(adam_flat.astype(jnp.bfloat16), ("dp", "shard"), axis=0, tiled=True)
    slot_low = lax.all_gather(blocks_w.astype(jnp.bfloat16), "shard", axis=0, tiled=True)
    block_ids = jnp.arange(NBLK, dtype=jnp.int32)
    slot_of = jnp.sum(
        block_ids[:, None] * (owner_map[:, None] == block_ids[None, :]).astype(jnp.int32), axis=0
    )
    blocks = jnp.take(slot_low, slot_of, axis=0)
    w_qkv = jnp.concatenate([blocks[0], blocks[1], blocks[2]], axis=1)
    w_proj = blocks[3]
    w_up = jnp.concatenate([blocks[4 + which] for which in range(fc_ratio)], axis=1)
    w_down = blocks[4 + fc_ratio :].reshape(F, D)
    pieces_low = unflatten(flat_low)
    pieces = [piece.astype(jnp.float32) for piece in pieces_low]
    (
        patch_weight,
        patch_bias,
        time_in_weight,
        time_in_bias,
        time_out_weight,
        time_out_bias,
        class_table,
        mod_weight,
        mod_bias,
        query_bias,
        value_bias,
        proj_bias,
        hidden_bias,
        down_bias,
        final_mod_weight,
        final_mod_bias,
        final_weight,
        final_bias,
        align_weight,
        align_bias,
    ) = pieces
    patch_low = pieces_low[0]
    final_low = pieces_low[16]
    align_low = pieces_low[18]
    cond_weights = (
        time_in_weight,
        time_in_bias,
        time_out_weight,
        time_out_bias,
        class_table,
        mod_weight,
        mod_bias,
        final_mod_weight,
        final_mod_bias,
    )
    (modulation, final_mods), cond_back = jax.vjp(
        functools.partial(condition_terms, tstep_idx, class_ids), *cond_weights
    )
    shift_one, scale_one, gate_one, shift_two, scale_two, gate_two = [
        modulation[:, None, which * D : (which + 1) * D] for which in range(6)
    ]
    final_shift = final_mods[:, None, :D]
    final_scale = final_mods[:, None, D:]
    noisy_low = noisy.astype(jnp.bfloat16).reshape(rows, PD)
    hidden0 = (matmul(noisy_low, patch_low) + patch_bias).reshape(images, seq, D) + position_table()
    norm_one, inv_one = normalize(hidden0)
    act_one = (norm_one * (1.0 + scale_one) + shift_one).astype(jnp.bfloat16).reshape(rows, D)
    qkv_bias = jnp.concatenate([query_bias, jnp.zeros((D,), jnp.float32), value_bias])
    projected = (
        (matmul(act_one, w_qkv) + qkv_bias)
        .astype(jnp.bfloat16)
        .reshape(images, seq, 3, HEADS, HDIM)
    )
    queries = projected[:, :, 0]
    key_part = projected[:, :, 1]
    values = projected[:, :, 2]
    scale_qk = HDIM ** (-0.5)
    scores = (
        jnp.einsum("gqhe,gkhe->ghqk", queries, key_part, preferred_element_type=jnp.float32)
        * scale_qk
    )
    row_max = jnp.max(scores, axis=-1, keepdims=True)
    log_total = row_max + jnp.log(jnp.sum(jnp.exp(scores - row_max), axis=-1, keepdims=True))
    probs_low = jnp.exp(scores - log_total).astype(jnp.bfloat16)
    attended = (
        jnp.einsum("ghqk,gkhe->gqhe", probs_low, values, preferred_element_type=jnp.float32)
        .reshape(rows, D)
        .astype(jnp.bfloat16)
    )
    branch_one = (matmul(attended, w_proj) + proj_bias).reshape(images, seq, D)
    hidden1 = hidden0 + gate_one * branch_one
    norm_two, inv_two = normalize(hidden1)
    act_two = (norm_two * (1.0 + scale_two) + shift_two).astype(jnp.bfloat16).reshape(rows, D)
    inner_pre = matmul(act_two, w_up) + hidden_bias
    gelu_out, gelu_back = jax.vjp(functools.partial(jax.nn.gelu, approximate=True), inner_pre)
    gelu_low = gelu_out.astype(jnp.bfloat16)
    branch_two = (matmul(gelu_low, w_down) + down_bias).reshape(images, seq, D)
    hidden2 = hidden1 + gate_two * branch_two
    norm_three, inv_three = normalize(hidden2)
    act_three = (
        (norm_three * (1.0 + final_scale) + final_shift).astype(jnp.bfloat16).reshape(rows, D)
    )
    output = (matmul(act_three, final_low) + final_bias).reshape(images, seq, PD)
    errors = output - velocity
    main_term = jnp.sum(time_weight[:, None, None] * errors * errors) / (total_img * SEQ * PD)
    hidden1_low = hidden1.astype(jnp.bfloat16).reshape(rows, D)
    aligned = matmul(hidden1_low, align_low) + align_bias
    dino_f = dino.astype(jnp.float32).reshape(rows, DINO)
    cosine_sum, cosine_back = jax.vjp(functools.partial(cosine_total, dino_f=dino_f), aligned)
    align_scale = REPA_WEIGHT / (total_img * SEQ)
    loss_local = main_term - align_scale * cosine_sum
    back_output = (
        (2.0 * time_weight[:, None, None] * errors / (total_img * SEQ * PD))
        .reshape(rows, PD)
        .astype(jnp.bfloat16)
    )
    grad_final = matmul(act_three.T, back_output)
    grad_final_bias = row_total(back_output)
    back_three = matmul(back_output, final_low.T).reshape(images, seq, D)
    grad_final_shift = jnp.sum(back_three, axis=1)
    grad_final_scale = jnp.sum(back_three * norm_three, axis=1)
    back_hidden2 = normalize_back(back_three * (1.0 + final_scale), norm_three, inv_three)
    back_branch_two = (back_hidden2 * gate_two).reshape(rows, D).astype(jnp.bfloat16)
    grad_gate_two = jnp.sum(back_hidden2 * branch_two, axis=1)
    grad_down = matmul(gelu_low.T, back_branch_two)
    grad_down_bias = row_total(back_branch_two)
    back_inner = gelu_back(matmul(back_branch_two, w_down.T))[0].astype(jnp.bfloat16)
    grad_up = matmul(act_two.T, back_inner)
    grad_hidden_bias = row_total(back_inner)
    back_two = matmul(back_inner, w_up.T).reshape(images, seq, D)
    grad_shift_two = jnp.sum(back_two, axis=1)
    grad_scale_two = jnp.sum(back_two * norm_two, axis=1)
    back_aligned = cosine_back(jnp.asarray(-align_scale, jnp.float32))[0].astype(jnp.bfloat16)
    grad_align = matmul(hidden1_low.T, back_aligned)
    grad_align_bias = row_total(back_aligned)
    back_hidden1 = (
        back_hidden2
        + normalize_back(back_two * (1.0 + scale_two), norm_two, inv_two)
        + matmul(back_aligned, align_low.T).reshape(images, seq, D)
    )
    back_branch_one = (back_hidden1 * gate_one).reshape(rows, D).astype(jnp.bfloat16)
    grad_gate_one = jnp.sum(back_hidden1 * branch_one, axis=1)
    grad_proj = matmul(attended.T, back_branch_one)
    grad_proj_bias = row_total(back_branch_one)
    back_attended = (
        matmul(back_branch_one, w_proj.T).astype(jnp.bfloat16).reshape(images, seq, HEADS, HDIM)
    )
    back_probs = jnp.einsum(
        "gqhe,gkhe->ghqk", back_attended, values, preferred_element_type=jnp.float32
    )
    grad_values = jnp.einsum(
        "ghqk,gqhe->gkhe", probs_low, back_attended, preferred_element_type=jnp.float32
    )
    scores_again = (
        jnp.einsum("gqhe,gkhe->ghqk", queries, key_part, preferred_element_type=jnp.float32)
        * scale_qk
    )
    probs_again = jnp.exp(scores_again - log_total)
    back_scores = (
        probs_again * (back_probs - jnp.sum(back_probs * probs_again, axis=-1, keepdims=True))
    ).astype(jnp.bfloat16)
    grad_queries = (
        jnp.einsum("ghqk,gkhe->gqhe", back_scores, key_part, preferred_element_type=jnp.float32)
        * scale_qk
    )
    grad_keys = (
        jnp.einsum("ghqk,gqhe->gkhe", back_scores, queries, preferred_element_type=jnp.float32)
        * scale_qk
    )
    back_projected = (
        jnp.stack([grad_queries, grad_keys, grad_values], axis=2)
        .reshape(rows, 3 * D)
        .astype(jnp.bfloat16)
    )
    grad_qkv = matmul(act_one.T, back_projected)
    grad_qkv_bias = row_total(back_projected)
    back_one = matmul(back_projected, w_qkv.T).reshape(images, seq, D)
    grad_shift_one = jnp.sum(back_one, axis=1)
    grad_scale_one = jnp.sum(back_one * norm_one, axis=1)
    back_hidden0 = (
        (back_hidden1 + normalize_back(back_one * (1.0 + scale_one), norm_one, inv_one))
        .reshape(rows, D)
        .astype(jnp.bfloat16)
    )
    grad_patch = matmul(noisy_low.T, back_hidden0)
    grad_patch_bias = row_total(back_hidden0)
    grad_modulation = jnp.concatenate(
        [
            grad_shift_one,
            grad_scale_one,
            grad_gate_one,
            grad_shift_two,
            grad_scale_two,
            grad_gate_two,
        ],
        axis=1,
    )
    grad_final_mods = jnp.concatenate([grad_final_shift, grad_final_scale], axis=1)
    cond_grads = cond_back((grad_modulation, grad_final_mods))
    grad_list = (
        [grad_patch, grad_patch_bias]
        + list(cond_grads[:7])
        + [
            grad_qkv_bias[:D],
            grad_qkv_bias[2 * D :],
            grad_proj_bias,
            grad_hidden_bias,
            grad_down_bias,
            cond_grads[7],
            cond_grads[8],
            grad_final,
            grad_final_bias,
            grad_align,
            grad_align_bias,
        ]
    )
    flat_grad = jnp.concatenate(
        [gradient_part.reshape(-1) for gradient_part in grad_list]
        + [jnp.zeros((ADAM_PAD - ADAM_LEN,), jnp.float32)]
    )
    grad_model = jnp.concatenate(
        [
            grad_qkv.reshape(D, 3, D).transpose(1, 0, 2),
            grad_proj[None],
            grad_up.reshape(D, fc_ratio, D).transpose(1, 0, 2),
            grad_down.reshape(fc_ratio, D, D),
        ],
        axis=0,
    )
    grad_slot = jnp.take(grad_model, owner_map, axis=0)
    flat_owned = lax.psum_scatter(flat_grad, ("dp", "shard"), scatter_dimension=0, tiled=True)
    loss_total = lax.psum(loss_local, ("dp", "shard"))
    summed = lax.psum(grad_slot, "dp")
    owned = lax.psum_scatter(
        summed.astype(jnp.bfloat16), "shard", scatter_dimension=0, tiled=True
    ).astype(jnp.float32)
    new_left = STAT_BETA * stat_left + (1.0 - STAT_BETA) * jnp.einsum(
        "bij,bkj->bik", owned, owned, precision=HIGHEST
    )
    new_right = STAT_BETA * stat_right + (1.0 - STAT_BETA) * jnp.einsum(
        "bji,bjk->bik", owned, owned, precision=HIGHEST
    )
    left_applied = jnp.einsum("bij,bjk->bik", root_left, owned, precision=HIGHEST)
    direction = jnp.einsum("bij,bjk->bik", left_applied, root_right, precision=HIGHEST)
    root_mean = jnp.sqrt(jnp.mean(direction * direction, axis=(1, 2), keepdims=True))
    block_update = -SHAMPOO_RATE * (direction / (root_mean + RMS_EPS) + DECAY_RATE * blocks_w)
    new_m = BETA_ONE * adam_m + (1.0 - BETA_ONE) * flat_owned
    new_v = BETA_TWO * adam_v + (1.0 - BETA_TWO) * flat_owned * flat_owned
    corrected_m = new_m / (1.0 - BETA_ONE**STEP)
    corrected_v = new_v / (1.0 - BETA_TWO**STEP)
    adam_update = -ADAM_RATE * (
        corrected_m / (jnp.sqrt(corrected_v) + ADAM_EPS) + DECAY_RATE * adam_flat
    )
    return (loss_total, block_update, new_left, new_right, adam_update, new_m, new_v)


def solution(mesh):
    return jax.shard_map(
        body,
        mesh=mesh,
        in_specs=(
            P(("dp", "shard"), None, None),
            P(("dp", "shard"), None, None),
            P(("dp", "shard")),
            P(("dp", "shard")),
            P(("dp", "shard")),
            P(("dp", "shard"), None, None),
            P(),
            P(("dp", "shard")),
            P(("dp", "shard")),
            P(("dp", "shard")),
            P("shard", None, None),
            P("shard", None, None),
            P("shard", None, None),
            P("shard", None, None),
            P("shard", None, None),
        ),
        out_specs=(
            P(),
            P("shard", None, None),
            P("shard", None, None),
            P("shard", None, None),
            P(("dp", "shard")),
            P(("dp", "shard")),
            P(("dp", "shard")),
        ),
        check_vma=False,
    )
```

profile of v0, /device:TPU:0, one launch (start us, length us, event | category | flops | bytes accessed | tf_op | source)
XLA Modules:
  0.0 797.5 jit_solution(3456417252762726016)
XLA Ops:
  17.3 26.3 %all-gather.5.cloned.1.call-done = bf16[12,384,384]{2,1,0:T(8,128)(2,1)} async-done(((bf16[3,384,384]{2,1,0:T(8,128)(2,1)}), bf16[12,384,384]{2,1,0:T(8,128)(2,1)}) %all-gather.5.cloned.1.call-update) | async-done | bytes 3538960 | tf_op jit(solution)/shard_map/all_gather | solution.py:172
  43.6 5.1 gather_fusion
  54.7 54.4 %all-gather.3.cloned.1.call-done = bf16[2129920]{0:T(1024)(128)(2,1)} async-done(((bf16[66560]{0:T(1024)(128)(2,1)}), bf16[2129920]{0:T(1024)(128)(2,1)}) %all-gather.3.cloned.1.call-update) | async-done | bytes 4259856 | tf_op jit(solution)/shard_map/all_gather | solution.py:171
  122.9 3.3 reshape.435
  140.5 4.3 copy.90
  144.9 6.1 reshape.436
  159.4 3.6 fusion.106
  169.8 3.8 fusion.104
  182.8 2.9 multiply_reduce_fusion.7
  188.0 7.3 fusion.13
  195.3 5.1 convert_reduce_fusion
  200.5 3.1 fusion.33
  203.7 3.5 multiply_reduce_fusion.2
  210.2 3.0 convert_reduce_fusion.4
  221.7 7.7 multiply_reduce_fusion
  229.4 6.3 multiply_convert_fusion
  252.4 4.8 fusion.95
  265.5 3.4 fusion.46
  271.7 3.4 copy.104
  276.5 4.7 reshape.451
  300.5 87.2 %concatenate.35 = f32[2129920]{0:T(1024)} concatenate(f32[6144]{0:T(1024)} %reshape.447, f32[384]{0:T(512)} %get-tuple-element.39, f32[98304]{0:T(1024)S(1)} %copy-done.57, f32[384]{0:T(512)} %get-tuple-element.37, f32[147456]{0:T(1024)S(1)} %reshape.449, f32[384]{0:T(512)} %get-tuple-element.110, f32[384384]{0:T(1024)} %reshape.450, f32[884736]{0:T(1024)} %reshape.451, ...), dimensions={0} | concatenate | bytes 17039360 | tf_op jit(solution)/shard_map/concatenate | solution.py:381
  391.3 4.9 copy.131
  396.2 5.1 convolution_bitcast_fusion
  401.3 4.7 copy.132
  406.1 4.2 fusion.114
  410.3 3.3 pad_maximum_fusion
  413.5 7.0 gather_fusion.1
  420.6 6.6 broadcast_select_fusion
  427.1 306.0 %all-reduce.5 = bf16[12,384,384]{2,1,0:T(8,128)(2,1)} all-reduce(f32[12,384,384]{2,1,0:T(8,128)} %broadcast_select_fusion), channel_id=1, replica_groups=mesh['dp'=8,'shard'=4] {'dp'}, use_global_device_ids=true, to_apply=%region_20.21 | all-reduce | flops 1769472 | bytes 10616832 | tf_op jit(solution)/shard_map/psum | solution.py:397
  734.7 40.7 %psum.14 = f32[]{:T(128)} all-reduce(f32[]{:T(128)S(6)} %sub.143), channel_id=1, replica_groups=mesh['dp'=8,'shard'=4] {'dp','shard'}, use_global_device_ids=true, to_apply=%region_14.15 | all-reduce | flops 1 | bytes 8 | tf_op jit(solution)/shard_map/psum | solution.py:396
  777.5 3.0 fusion.115
  780.6 3.8 multiply_reduce_fusion.3
  (360 shorter events, 142.5 us)
Async XLA Ops:
  7.2 773.4 %copy-start = (f32[3,384,384]{2,1,0:T(8,128)S(1)}, f32[3,384,384]{2,1,0:T(8,128)}, u32[]{:S(2)}) copy-start(f32[3,384,384]{2,1,0:T(8,128)} %param.29) | copy-start | bytes 5308420
  7.2 5.1 copy-start.22
  7.2 36.4 %all-gather.5.cloned.1.call-start = ((), (), s32[]{:S(2)}) async-start(), calls=%async_computation.2 | async-start | bytes 4423680 | tf_op jit(solution)/shard_map/all_gather | solution.py:172
  9.9 99.2 %all-gather.3.cloned.1.call-start = ((), (), s32[]{:S(2)}) async-start(), calls=%async_computation.1 | async-start | bytes 4392960 | tf_op jit(solution)/shard_map/all_gather | solution.py:171
  11.6 5.1 copy-start.98
  11.6 5.1 copy-start.96
  11.6 763.7 %all-reduce.4.cloned.1.call-start = ((), (), s32[]{:S(2)}) async-start(), calls=%async_computation.4 | async-start | bytes 17039360
  17.3 114.4 %copy-start.88 = (f32[4,128]{1,0:T(4,128)}, f32[4,128]{1,0:T(4,128)S(1)}, u32[]{:S(2)}) copy-start(f32[4,128]{1,0:T(4,128)S(1)} %get-tuple-element.90) | copy-start | bytes 6148
  17.3 114.4 %copy-start.90 = (f32[4,128]{1,0:T(4,128)}, f32[4,128]{1,0:T(4,128)S(1)}, u32[]{:S(2)}) copy-start(f32[4,128]{1,0:T(4,128)S(1)} %get-tuple-element.91) | copy-start | bytes 6148
  169.8 6.8 copy-start.82
  178.0 4.8 copy-start.91
  180.8 7.1 slice-start.2
  182.8 5.2 slice-start.3
  188.0 7.3 copy-start.66
  195.3 5.1 copy-start.3
  195.3 5.1 copy-start.59
  195.3 5.1 copy-start.61
  195.3 5.1 copy-start.63
  195.3 5.1 copy-start.65
  221.7 17.5 %slice-start = ((s8[6291456]{0:T(1024)(128)(4,1)}), s8[4194304]{0:T(1024)(128)(4,1)S(1)}, s32[]{:S(2)}) async-start(s8[6291456]{0:T(1024)(128)(4,1)} %bitcast.283), calls=%async_computation.5 | async-start | bytes 8388608
  229.4 6.4 copy-start.26
  229.4 9.8 %slice-start.1 = ((s8[6291456]{0:T(1024)(128)(4,1)}), s8[2097152]{0:T(1024)(128)(4,1)S(1)}, s32[]{:S(2)}) async-start(s8[6291456]{0:T(1024)(128)(4,1)} %bitcast.283), calls=%async_computation.6 | async-start | bytes 4194304
  252.4 5.3 copy-start.18
  257.7 6.1 copy-start.50
  257.7 7.7 copy-start.4
  265.5 6.2 copy-start.16
  282.4 8.4 %copy-start.38 = (f32[384,768]{1,0:T(8,128)S(1)}, f32[384,768]{1,0:T(8,128)}, u32[]{:S(2)}) copy-start(f32[384,768]{1,0:T(8,128)} %fusion.46) | copy-start | bytes 3538948
  291.9 6.4 copy-start.33
  291.9 8.6 %copy-start.57 = (f32[98304]{0:T(1024)S(1)}, f32[98304]{0:T(1024)}, u32[]{:S(2)}) copy-start(f32[98304]{0:T(1024)} %reshape.448) | copy-start | bytes 1179652
  387.7 389.8 %reduce-scatter.2.cloned.1.call-start = ((), (), s32[]{:S(2)}) async-start(), calls=%async_computation.3 | async-start | bytes 4423680 | tf_op jit(solution)/shard_map/reduce_scatter | solution.py:398
  413.5 7.0 copy-start.95
  733.2 44.4 %copy-start.54 = (f32[3,384,384]{2,1,0:T(8,128)S(1)}, f32[3,384,384]{2,1,0:T(8,128)}, u32[]{:S(2)}) copy-start(f32[3,384,384]{2,1,0:T(8,128)} %param.28) | copy-start | bytes 5308420
  (75 other events, 205.8 us)
Sparse Core Ops, SparseCore 0:
  10.1 33.4 all-gather.4
  47.1 61.9 all-gather.2
  387.8 243.0 all-reduce.3
  733.3 39.5 reduce-scatter.1
where the time goes:
time: 810 us; the launch traced here: 798 us
  blocking collectives  347 us (43%)
  local copies, waits for them, and re-layouts  186 us (23%)
  matrix products  103 us (13%)
  waiting for transfers between devices  80.8 us (10%)
  other arithmetic  64.9 us (8%)
  between operations  16.6 us (2%)
    psum x1, blocking collectives, body(): summed = lax.psum(grad_slot, 'dp')  306 us
    concatenate x1, local copies, waits for them, and re-layouts, body(): jnp.concatenate([gradient_part.reshape(-1) for gradient_part in grad_list...  87.2 us
    dot_general x20, matrix products, matmul(): return jnp.dot(left, right, preferred_element_type=jnp.float32)  57.1 us
    all_gather x1, waiting for transfers between devices, body(): lax.all_gather(adam_flat.astype(jnp.bfloat16), ('dp', 'shard'), axis=0, t...  54.4 us
    psum x1, blocking collectives, body(): loss_total = lax.psum(loss_local, ('dp', 'shard'))  40.7 us
    all_gather x1, waiting for transfers between devices, body(): lax.all_gather(blocks_w.astype(jnp.bfloat16), 'shard', axis=0, tiled=True)  26.3 us
  transfers between devices with their start and end apart: 4, of which 2 were waited for; matrix products, arithmetic and copies ran while one was open for 7% of the time, Pallas kernels for 0%

commit v1 on v0

--- a/solution.py
+++ b/solution.py
@@ -168,7 +168,21 @@
     total_img = images * devices
     rows = images * seq
     fc_ratio = F // D
-    flat_low = lax.all_gather(adam_flat.astype(jnp.bfloat16), ("dp", "shard"), axis=0, tiled=True)
+
+    def see_column(piece_in, named_axis):
+        newest, later = (lax.axis_size(named_axis), lax.axis_index(named_axis))
+        w2, t1 = (piece_in, 1)
+        while t1 < newest:
+            formed = lax.ppermute(
+                w2, named_axis, list(map(lambda rr: (rr, rr ^ t1), range(newest)))
+            )
+            then = jnp.concatenate([w2, formed], axis=0)
+            current_arr = jnp.concatenate([formed, w2], axis=0)
+            w2 = jnp.where(later & t1 == 0, then, current_arr)
+            t1 = 2 * t1
+        return w2
+
+    flat_low = see_column(adam_flat.astype(jnp.bfloat16), ("dp", "shard"))
     slot_low = lax.all_gather(blocks_w.astype(jnp.bfloat16), "shard", axis=0, tiled=True)
     block_ids = jnp.arange(NBLK, dtype=jnp.int32)
     slot_of = jnp.sum(

time: 810 us -> 939 us (1.16)
  local copies, waits for them, and re-layouts: 186 us -> 269 us
  other arithmetic: 64.9 us -> 91.6 us
  waiting for transfers between devices: 80.8 us -> 92.9 us
    ppermute x0 -> x5, waiting for transfers between devices: none -> 92.8 us  [see_column(): lax.ppermute(w2, named_axis, list(map(lambda rr: (rr, rr ^ t1), range(new...]
    concatenate x0 -> x10, local copies, waits for them, and re-layouts: none -> 62.5 us  [see_column(): then = jnp.concatenate([w2, formed], axis=0)]
    all_gather x1 -> x0, waiting for transfers between devices: 54.4 us -> none  [body(): lax.all_gather(adam_flat.astype(jnp.bfloat16), ('dp', 'shard'), axis=0, t...]
    select_n x0 -> x9, other arithmetic: none -> 28.8 us  [see_column(): w2 = jnp.where(later & t1 == 0, then, current_arr)]
    all_gather x1, waiting for transfers between devices: 26.3 us -> 0.01 us  [body(): lax.all_gather(blocks_w.astype(jnp.bfloat16), 'shard', axis=0, tiled=True)]
    reshape x0 -> x3, local copies, waits for them, and re-layouts: none -> 9.75 us  [the longest x1 3.59 us: body(): (matmul(noisy_low, patch_low) + patch_bias).reshape(images, seq, D)]
  transfers between devices with their start and end apart: 4 -> 8, of which waited for: 2 -> 4; matrix products, arithmetic and copies ran while one was open for 7% -> 19% of each run, Pallas kernels for 0% -> 0%
where the time goes in v1:
time: 939 us; the launch traced here: 929 us
  blocking collectives  348 us (37%)
  local copies, waits for them, and re-layouts  269 us (29%)
  matrix products  103 us (11%)
  waiting for transfers between devices  92.9 us (10%)
  other arithmetic  91.6 us (10%)
  between operations  16.8 us (2%)
    psum x1, blocking collectives, body(): summed = lax.psum(grad_slot, 'dp')  309 us
    ppermute x5, waiting for transfers between devices, see_column(): lax.ppermute(w2, named_axis, list(map(lambda rr: (rr, rr ^ t1), range(new...  92.8 us
    concatenate x1, local copies, waits for them, and re-layouts, body(): jnp.concatenate([gradient_part.reshape(-1) for gradient_part in grad_list...  78.1 us
    concatenate x10, local copies, waits for them, and re-layouts, see_column(): then = jnp.concatenate([w2, formed], axis=0)  62.5 us
    dot_general x20, matrix products, matmul(): return jnp.dot(left, right, preferred_element_type=jnp.float32)  54.4 us
    psum x1, blocking collectives, body(): loss_total = lax.psum(loss_local, ('dp', 'shard'))  39.6 us
    select_n x9, other arithmetic, see_column(): w2 = jnp.where(later & t1 == 0, then, current_arr)  28.8 us
  transfers between devices with their start and end apart: 8, of which 4 were waited for; matrix products, arithmetic and copies ran while one was open for 19% of the time, Pallas kernels for 0%

profile of v1, /device:TPU:0, one launch (start us, length us, event | category | flops | bytes accessed | tf_op | source)
XLA Modules:
  0.0 929.3 jit_solution(3737484209795014844)
XLA Ops:
  41.1 6.4 collective-permute-done.2
  51.2 4.0 concatenate.110
  55.2 3.8 copy.174
  61.5 12.6 %collective-permute-done.3 = bf16[532480]{0:T(1024)(128)(2,1)S(1)} collective-permute-done((bf16[532480]{0:T(1024)(128)(2,1)}, bf16[532480]{0:T(1024)(128)(2,1)S(1)}, u32[]{:S(2)}, u32[]{:S(2)}) %collective-permute-start.3) | collective-permute-done | bytes 1064992 | tf_op jit(solution)/shard_map/ppermute | solution.py:176
  74.0 9.6 %maximum_select_fusion.2 = bf16[1064960]{0:T(1024)(128)(2,1)} fusion(bf16[532480]{0:T(1024)(128)(2,1)S(1)} %collective-permute-done.3, bf16[532480]{0:T(1024)(128)(2,1)} %maximum_select_fusion.4, pred[]{:T(512)S(6)} %eq.44), kind=kLoop, calls=%fused_computation.56 | loop fusion | flops 9584640 | bytes 4259841 | tf_op jit(solution)/shard_map/jit(_where)/select_n | solution.py:181
  86.1 7.4 concatenate.113
  93.5 7.1 copy.176
  104.0 72.3 %collective-permute-done.4 = bf16[1064960]{0:T(1024)(128)(2,1)} collective-permute-done((bf16[1064960]{0:T(1024)(128)(2,1)}, bf16[1064960]{0:T(1024)(128)(2,1)}, u32[]{:S(2)}, u32[]{:S(2)}) %collective-permute-start.4) | collective-permute-done | bytes 2129952 | tf_op jit(solution)/shard_map/ppermute | solution.py:176
  176.3 6.8 maximum_select_fusion
  190.1 17.6 %concatenate.116 = bf16[66560,16]{1,0:T(8,128)(2,1)} reshape(bf16[1064960]{0:T(1024)(128)(2,1)} %collective-permute-done.4) | data formatting | bytes 4259840 | tf_op jit(solution)/shard_map/concatenate | solution.py:179
  207.7 13.4 %copy.178 = bf16[66560,16]{0,1:T(8,128)(2,1)} copy(bf16[66560,16]{1,0:T(8,128)(2,1)} %concatenate.116) | data formatting | bytes 4259840 | tf_op jit(solution)/shard_map/concatenate | solution.py:179
  266.7 5.1 gather_fusion
  281.1 4.3 copy.157
  285.4 5.7 reshape.445
  309.7 4.3 fusion.98
  331.7 7.2 fusion.13
  338.9 5.1 convert_reduce_fusion
  371.3 4.4 convolution_bitcast_fusion.2
  375.8 7.2 multiply_reduce_fusion
  383.0 4.5 multiply_convert_fusion
  409.4 4.7 fusion.89
  420.8 4.8 copy.222
  425.5 4.7 copy.221
  430.3 4.8 convolution_bitcast_fusion
  445.3 4.6 reshape.460
  456.9 78.1 %concatenate.122 = f32[2129920]{0:T(1024)} concatenate(f32[6144]{0:T(1024)S(1)} %reshape.456, f32[384]{0:T(512)S(1)} %copy-done.114, f32[98304]{0:T(1024)} %reshape.457, f32[384]{0:T(512)S(1)} %copy-done.116, f32[147456]{0:T(1024)} %reshape.458, f32[384]{0:T(512)S(1)} %copy-done.115, f32[384384]{0:T(1024)S(1)} %copy-done.45, f32[884736]{0:T(1024)} %reshape.460, ...), dimensions={0} | concatenate | bytes 17039360 | tf_op jit(solution)/shard_map/concatenate | solution.py:395
  536.1 3.8 fusion.105
  543.3 7.5 gather_fusion.1
  550.8 6.7 broadcast_select_fusion
  557.4 308.7 %all-reduce.5 = bf16[12,384,384]{2,1,0:T(8,128)(2,1)} all-reduce(f32[12,384,384]{2,1,0:T(8,128)} %broadcast_select_fusion), channel_id=1, replica_groups=mesh['dp'=8,'shard'=4] {'dp'}, use_global_device_ids=true, to_apply=%region_20.21 | all-reduce | flops 1769472 | bytes 10616832 | tf_op jit(solution)/shard_map/psum | solution.py:411
  867.5 39.6 %psum.14 = f32[]{:T(128)} all-reduce(f32[]{:T(128)S(6)} %sub.143), channel_id=1, replica_groups=mesh['dp'=8,'shard'=4] {'dp','shard'}, use_global_device_ids=true, to_apply=%region_14.15 | all-reduce | flops 1 | bytes 8 | tf_op jit(solution)/shard_map/psum | solution.py:410
  912.3 3.8 multiply_reduce_fusion.3
  (472 shorter events, 231.6 us)
Async XLA Ops:
  7.2 905.1 %copy-start = (f32[3,384,384]{2,1,0:T(8,128)S(1)}, f32[3,384,384]{2,1,0:T(8,128)}, u32[]{:S(2)}) copy-start(f32[3,384,384]{2,1,0:T(8,128)} %param.29) | copy-start | bytes 5308420
  7.2 259.6 %all-gather.2.cloned.1.call-start = ((), (), s32[]{:S(2)}) async-start(), calls=%async_computation.1 | async-start | bytes 4423680 | tf_op jit(solution)/shard_map/all_gather | solution.py:186
  8.3 6.3 copy-start.125
  8.4 6.8 copy-start.11
  8.4 9.0 collective-permute-start
  11.4 895.7 %all-reduce.4.cloned.1.call-start = ((), (), s32[]{:S(2)}) async-start(), calls=%async_computation.3 | async-start | bytes 17039360
  17.4 8.3 copy-start.37
  18.6 14.6 %collective-permute-start.1 = (bf16[133120]{0:T(1024)(128)(2,1)S(1)}, bf16[133120]{0:T(1024)(128)(2,1)S(1)}, u32[]{:S(2)}, u32[]{:S(2)}) collective-permute-start(bf16[133120]{0:T(1024)(128)(2,1)S(1)} %maximum_select_fusion.7), channel_id=1, source_target_pairs={{0,2},{1,3},{2,0},{3,1},{4,6},{5,7},{6,4},{7,5},{8,10},{9,11},{10,... | collective-permute-start | bytes 798728 | tf_op jit(solution)/shard_map/ppermute | solution.py:176
  27.0 205.3 %copy-start.99 = (f32[4,128]{1,0:T(4,128)}, f32[4,128]{1,0:T(4,128)S(1)}, u32[]{:S(2)}) copy-start(f32[4,128]{1,0:T(4,128)S(1)} %get-tuple-element.90) | copy-start | bytes 6148
  27.0 205.3 %copy-start.101 = (f32[4,128]{1,0:T(4,128)}, f32[4,128]{1,0:T(4,128)S(1)}, u32[]{:S(2)}) copy-start(f32[4,128]{1,0:T(4,128)S(1)} %get-tuple-element.91) | copy-start | bytes 6148
  34.1 13.4 %collective-permute-start.2 = (bf16[266240]{0:T(1024)(128)(2,1)}, bf16[266240]{0:T(1024)(128)(2,1)S(1)}, u32[]{:S(2)}, u32[]{:S(2)}) collective-permute-start(bf16[266240]{0:T(1024)(128)(2,1)} %maximum_select_fusion.6), channel_id=1, source_target_pairs={{0,4},{1,5},{2,6},{3,7},{4,0},{5,1},{6,2},{7,3},{8,12},{9,13},{10,... | collective-permute-start | bytes 1597448 | tf_op jit(solution)/shard_map/ppermute | solution.py:176
  50.0 24.1 %collective-permute-start.3 = (bf16[532480]{0:T(1024)(128)(2,1)}, bf16[532480]{0:T(1024)(128)(2,1)S(1)}, u32[]{:S(2)}, u32[]{:S(2)}) collective-permute-start(bf16[532480]{0:T(1024)(128)(2,1)} %maximum_select_fusion.4), channel_id=1, source_target_pairs={{0,8},{1,9},{2,10},{3,11},{4,12},{5,13},{6,14},{7,15},{8,0},{9,1},... | collective-permute-start | bytes 3194888 | tf_op jit(solution)/shard_map/ppermute | solution.py:176
  83.7 92.7 %collective-permute-start.4 = (bf16[1064960]{0:T(1024)(128)(2,1)}, bf16[1064960]{0:T(1024)(128)(2,1)}, u32[]{:S(2)}, u32[]{:S(2)}) collective-permute-start(bf16[1064960]{0:T(1024)(128)(2,1)} %maximum_select_fusion.2), channel_id=1, source_target_pairs={{0,16},{1,17},{2,18},{3,19},{4,20},{5,21},{6,22},{7,23},{8,24},{9,... | collective-permute-start | bytes 6389768 | tf_op jit(solution)/shard_map/ppermute | solution.py:176
  207.7 13.4 %copy-start.51 = (bf16[294912]{0:T(1024)(128)(2,1)S(1)}, bf16[294912]{0:T(1024)(128)(2,1)}, u32[]{:S(2)}) copy-start(bf16[294912]{0:T(1024)(128)(2,1)} %get-tuple-element.53) | copy-start | bytes 1769476
  228.8 9.5 %copy-start.8 = (bf16[384,2304]{1,0:T(8,128)(2,1)}, bf16[384,2304]{1,0:T(8,128)(2,1)S(1)}, u32[]{:S(2)}) copy-start(bf16[384,2304]{1,0:T(8,128)(2,1)S(1)} %reshape.444) | copy-start | bytes 5308420
  257.9 7.4 copy-start.2
  266.7 5.1 copy-start.124
  327.0 17.0 %copy-start.4 = (f32[4,256,384]{2,1,0:T(8,128)}, f32[4,256,384]{2,1,0:T(8,128)S(1)}, u32[]{:S(2)}) copy-start(f32[4,256,384]{2,1,0:T(8,128)S(1)} %multiply_add_fusion.2) | copy-start | bytes 4718596
  331.7 7.2 copy-start.68
  338.9 5.2 copy-start.59
  338.9 5.2 copy-start.61
  338.9 5.2 copy-start.63
  338.9 5.2 copy-start.65
  338.9 5.2 copy-start.93
  338.9 5.2 copy-start.94
  371.3 11.6 %slice-start = ((s8[6291456]{0:T(1024)(128)(4,1)}), s8[4194304]{0:T(1024)(128)(4,1)S(1)}, s32[]{:S(2)}) async-start(s8[6291456]{0:T(1024)(128)(4,1)} %bitcast.248), calls=%async_computation.4 | async-start | bytes 8388608
  375.8 7.2 slice-start.1
  401.8 5.4 copy-start.122
  438.7 5.4 copy-start.44
  535.0 374.3 %reduce-scatter.2.cloned.1.call-start = ((), (), s32[]{:S(2)}) async-start(), calls=%async_computation.2 | async-start | bytes 4423680 | tf_op jit(solution)/shard_map/reduce_scatter | solution.py:412
  543.3 7.5 copy-start.123
  866.2 43.1 %copy-start.53 = (f32[3,384,384]{2,1,0:T(8,128)S(1)}, f32[3,384,384]{2,1,0:T(8,128)}, u32[]{:S(2)}) copy-start(f32[3,384,384]{2,1,0:T(8,128)} %param.28) | copy-start | bytes 5308420
  (110 other events, 271.7 us)
Sparse Core Ops, SparseCore 0:
  11.6 37.1 all-gather.1
  535.2 271.5 all-reduce.3
  866.3 39.6 reduce-scatter.1
